TPU v7x, 32 devices: a whole 2x2x4 slice. The times are simulated.
32 devices in a mesh: dp: 8 (over z, y), mp: 4 (over x, core).
Axes of the slice: x: 2, y: 2, z: 4, core: 2. Of those that a mesh axis runs over, the one named last changes fastest.
Arguments:
- embedded: bfloat16 [32, 64, 4096], P('dp', None, 'mp'), may hold values from -6 to 6
- targets: int32 [32, 64], P('dp'), may hold values from 0 to 65535
- labels: int32 [32], P('dp'), may hold values from 0 to 21
- counts: int32 [8], replicated, may hold values from 0 to 4, as said below
- destinations: int32 [32], P('dp'), may hold values from 0 to 15, as said below
- gain_in: float32 [4096], replicated, may hold values from 0.1 to 1.9
- w_query: bfloat16 [4096, 2048], P(None, 'mp'), may hold values from -40 to 40
- w_key: bfloat16 [4096, 1024], P(None, 'mp'), may hold values from -0.09375 to 0.09375
- w_value: bfloat16 [4096, 1024], P(None, 'mp'), may hold values from -0.09375 to 0.09375
- w_out: bfloat16 [2048, 4096], P('mp'), may hold values from -0.5 to 0.5
- gain_out: float32 [4096], replicated, may hold values from 0.1 to 1.9
- w_vocab: bfloat16 [4096, 65536], P('mp', 'dp'), may hold values from -40 to 40
- prev_probs: float32 [22], replicated, may hold values from 0.03 to 0.2
- log_weights: float32 [22], replicated, may hold values from -200 to 21000
Outputs:
- token_loss: float32 [1024], P(('dp', 'mp'))
- new_weights: float32 [22], replicated
- probs: float32 [22], replicated
Inputs may be any that keep to these rules, and one draw needn't show every extreme that they name: The counts sum to 16. `destinations`: each value from 0 to 15 is held by exactly one live slot; entries of slots that are not live are meaningless.
All inputs are finite; a program needn't handle non-finite values.
Results may differ from a plain program's by a relative error of at most 0.015.
The roundings to bfloat16 on the way count: a program that leaves them out, or rounds other values in their place, can miss the bound.
Values may be sent and summed in bfloat16 or wider, within the bound.
A program may use at most 192 MiB of HBM per device.

v0:
```python
import jax
import jax.numpy as jnp
from jax import lax
from jax.sharding import PartitionSpec as P

HEAD_DIM = 128
DOMAINS = 22
SEQ_DEV = 2
norm_eps = 1e-05
rope_base = 500000.0
memory_rate = 0.9
step_rate = 0.02
explore_mass = 0.005


def normalize(values, gain_vec):
    inv_rms = lax.rsqrt(jnp.mean(values * values, axis=-1, keepdims=True) + norm_eps)
    return values * inv_rms * gain_vec


def rotate_halves(tensor):
    full_width = tensor.shape[-1]
    half_width = full_width // 2
    frequency = jnp.power(
        jnp.float32(rope_base), -jnp.arange(half_width, dtype=jnp.float32) * 2.0 / full_width
    )
    angles = jnp.arange(tensor.shape[1], dtype=jnp.float32)[:, None] * frequency[None, :]
    cosine = jnp.cos(angles)[None, :, None, :]
    sine_part = jnp.sin(angles)[None, :, None, :]
    first_half = tensor[..., :half_width]
    second = tensor[..., half_width:]
    return jnp.concatenate(
        [first_half * cosine - second * sine_part, second * cosine + first_half * sine_part],
        axis=-1,
    )


def local(
    embedded,
    targets,
    labels,
    counts,
    destinations,
    gain_in,
    w_query,
    w_key,
    w_value,
    w_out,
    gain_out,
    w_vocab,
    prev_probs,
    log_weights,
):
    data_count = lax.axis_size("dp")
    data_index = lax.axis_index("dp")
    model_shard_count = lax.axis_size("mp")
    model_index = lax.axis_index("mp")
    slot_count = embedded.shape[0]
    seq_len = embedded.shape[1]
    seq_held = SEQ_DEV
    gathered_rows = (
        lax.all_gather(embedded, "dp", axis=0, tiled=True),
        lax.all_gather(targets, "dp", axis=0, tiled=True),
        lax.all_gather(labels, "dp", axis=0, tiled=True),
        lax.all_gather(destinations, "dp", axis=0, tiled=True),
    )
    slot_ids = jnp.arange(data_count * slot_count, dtype=jnp.int32)
    is_live = slot_ids % slot_count < counts[slot_ids // slot_count]
    wanted = data_index * seq_held + jnp.arange(seq_held, dtype=jnp.int32)
    picking_mask = (gathered_rows[3][None, :] == wanted[:, None]) & is_live[None, :]
    sequence_rows = jnp.einsum(
        "av,vyr->ayr",
        picking_mask.astype(jnp.bfloat16),
        gathered_rows[0],
        preferred_element_type=jnp.float32,
    ).astype(jnp.bfloat16)
    seq_targets = jnp.einsum("gs,sl->gl", picking_mask.astype(jnp.int32), gathered_rows[1])
    seq_labels = jnp.sum(jnp.where(picking_mask, gathered_rows[2][None, :], 0), axis=1).astype(
        jnp.int32
    )
    full_rows = lax.all_gather(sequence_rows, "mp", axis=2, tiled=True)
    rows_all = seq_held * seq_len
    flat_rows = full_rows.reshape(rows_all, -1).astype(jnp.float32)
    normed = normalize(flat_rows, gain_in).astype(jnp.bfloat16)
    local_heads = w_query.shape[1] // HEAD_DIM
    local_groups = w_key.shape[1] // HEAD_DIM
    query_heads = jnp.dot(normed, w_query, preferred_element_type=jnp.float32).reshape(
        seq_held, seq_len, local_heads, HEAD_DIM
    )
    key_heads = jnp.dot(normed, w_key, preferred_element_type=jnp.float32).reshape(
        seq_held, seq_len, local_groups, HEAD_DIM
    )
    value_heads = (
        jnp.dot(normed, w_value, preferred_element_type=jnp.float32)
        .astype(jnp.bfloat16)
        .reshape(seq_held, seq_len, local_groups, HEAD_DIM)
    )
    query_heads = rotate_halves(query_heads).astype(jnp.bfloat16)
    key_heads = rotate_halves(key_heads).astype(jnp.bfloat16)
    group_size = local_heads // local_groups
    key_heads = jnp.repeat(key_heads, group_size, axis=2)
    value_heads = jnp.repeat(value_heads, group_size, axis=2)
    scores = jnp.einsum(
        "sqhe,skhe->shqk", query_heads, key_heads, preferred_element_type=jnp.float32
    ) * HEAD_DIM ** (-0.5)
    causal = jnp.arange(seq_len)[:, None] >= jnp.arange(seq_len)[None, :]
    scores = jnp.where(causal[None, None], scores, -jnp.inf)
    weights = jax.nn.softmax(scores, axis=-1).astype(jnp.bfloat16)
    mixed_heads = jnp.einsum(
        "shqk,skhe->sqhe", weights, value_heads, preferred_element_type=jnp.float32
    )
    mixed_heads = mixed_heads.astype(jnp.bfloat16).reshape(rows_all, local_heads * HEAD_DIM)
    row_block_tiles = rows_all // model_shard_count
    update = lax.psum_scatter(
        jnp.dot(mixed_heads, w_out, preferred_element_type=jnp.float32).astype(jnp.bfloat16),
        "mp",
        scatter_dimension=0,
        tiled=True,
    ).astype(jnp.float32)
    my_start = model_index * row_block_tiles
    own_rows = lax.dynamic_slice_in_dim(flat_rows, my_start, row_block_tiles, 0)
    hidden = own_rows + update
    final_rows = normalize(hidden, gain_out).astype(jnp.bfloat16)
    own_targets = lax.dynamic_slice_in_dim(
        seq_targets.reshape(rows_all), my_start, row_block_tiles, 0
    )
    own_labels = lax.dynamic_slice_in_dim(
        jnp.repeat(seq_labels, seq_len), my_start, row_block_tiles, 0
    )
    everyone = (
        lax.all_gather(final_rows, "dp", axis=0, tiled=True),
        lax.all_gather(own_targets, "dp", axis=0, tiled=True),
        lax.all_gather(own_labels, "dp", axis=0, tiled=True),
    )
    all_rows = everyone[0]
    all_goals = everyone[1]
    all_kinds = everyone[2]
    vocab_local = w_vocab.shape[1]
    logits = jnp.dot(
        all_rows,
        lax.all_gather(w_vocab, "mp", axis=0, tiled=True),
        preferred_element_type=jnp.float32,
    )
    row_top = jnp.max(logits, axis=1)
    spread = jnp.sum(jnp.exp(logits - row_top[:, None]), axis=1)
    column_ids = all_goals - data_index * vocab_local
    picked = jnp.sum(
        jnp.where(
            jnp.arange(vocab_local, dtype=jnp.int32)[None, :] == column_ids[:, None], logits, 0.0
        ),
        axis=1,
    )
    top_all = lax.pmax(row_top, "dp")
    summed = lax.psum((spread * jnp.exp(row_top - top_all), picked), "dp")
    spread_all = summed[0]
    picked_all = summed[1]
    losses = top_all + jnp.log(spread_all) - picked_all
    own_loss = lax.dynamic_slice_in_dim(losses, data_index * row_block_tiles, row_block_tiles, 0)
    domains = jnp.arange(DOMAINS, dtype=jnp.int32)
    member = (all_kinds[:, None] == domains[None, :]).astype(jnp.float32)
    totals = lax.psum((jnp.sum(member * losses[:, None], axis=0), jnp.sum(member, axis=0)), "mp")
    loss_sums = totals[0]
    token_tally = totals[1]
    reward = loss_sums / jnp.maximum(token_tally, 1.0) / prev_probs
    new_weights = memory_rate * log_weights + (1.0 - memory_rate) * reward
    probs = (1.0 - DOMAINS * explore_mass) * jax.nn.softmax(step_rate * new_weights) + explore_mass
    return (own_loss, new_weights, probs)


def solution(mesh):
    placed = (
        P("dp", None, "mp"),
        P("dp", None),
        P("dp"),
        P(),
        P("dp"),
        P(),
        P(None, "mp"),
        P(None, "mp"),
        P(None, "mp"),
        P("mp", None),
        P(),
        P("mp", "dp"),
        P(),
        P(),
    )
    return jax.shard_map(
        local, mesh=mesh, in_specs=placed, out_specs=(P(("dp", "mp")), P(), P()), check_vma=False
    )
```

profile of v0, /device:TPU:0, one launch (start us, length us, event | category | flops | bytes accessed | tf_op | source)
XLA Modules:
  0.0 688.2 jit_solution(7423845925654693603)
XLA Ops:
  11.6 1.4 gather_fusion
  13.0 13.6 %all-reduce.5 = (s32[32]{0:T(128)S(1)}, s32[32]{0:T(128)S(1)}) all-reduce(s32[32]{0:T(128)S(1)} %dynamic-update-slice, s32[32]{0:T(128)S(1)} %dynamic-update-slice.2), channel_id=1, replica_groups=mesh['dp'=8,'mp'=4] {'dp'}, use_global_device_ids=true, to_apply=%add | all-reduce | flops 64 | bytes 512
  27.2 58.5 %all-gather.6.cloned.1.call-done = bf16[32,64,1024]{2,1,0:T(8,128)(2,1)} async-done(((bf16[4,64,1024]{2,1,0:T(8,128)(2,1)}), bf16[32,64,1024]{2,1,0:T(8,128)(2,1)}) %all-gather.6.cloned.1.call-update) | async-done | bytes 4194320 | tf_op jit(solution)/shard_map/all_gather | solution.py:62
  85.7 6.8 fusion.1
  93.3 4.1 copy.67
  97.5 6.5 copy.66
  104.1 4.5 all-gather.8.cloned.1.call-done
  108.7 1.5 multiply_reduce_fusion
  110.3 2.8 fusion.10
  113.2 3.7 fusion.12
  119.5 1.3 copy-done.1
  122.9 3.9 convolution_convert_fusion
  126.9 24.9 %reduce-scatter.2.cloned.1.call-done = bf16[32,4096]{1,0:T(8,128)(2,1)} async-done(((bf16[128,4096]{1,0:T(8,128)(2,1)}), bf16[32,4096]{1,0:T(8,128)(2,1)}) %reduce-scatter.2.cloned.1.call-update) | async-done | bytes 262160 | tf_op jit(solution)/shard_map/reduce_scatter | solution.py:114
  153.1 1.9 multiply_convert_fusion.3
  156.5 26.2 %all-gather = s32[8,4,64]{2,1,0:T(4,128)S(1)} all-gather(s32[1,4,64]{2,1,0:T(4,128)S(1)} %bitcast.56), channel_id=1, replica_groups=mesh['dp'=8,'mp'=4] {'dp'}, dimensions={0}, use_global_device_ids=true | all-gather | bytes 9216 | tf_op jit(solution)/shard_map/all_gather | solution.py:63
  183.2 10.0 %all-reduce.4 = (s32[256]{0:T(256)S(1)}, s32[256]{0:T(256)S(1)}) all-reduce(s32[256]{0:T(256)S(1)} %dynamic-slice_dynamic-update-slice_fusion.1, s32[256]{0:T(256)S(1)} %dynamic-slice_dynamic-update-slice_fusion), channel_id=1, replica_groups=mesh['dp'=8,'mp'=4] {'dp'}, use_global_device_ids=true, to_apply=%add.1 | all-reduce | flops 512 | bytes 4096
  193.3 11.1 %all-gather.10.cloned.1.call-done = bf16[256,4096]{1,0:T(8,128)(2,1)} async-done(((bf16[32,4096]{1,0:T(8,128)(2,1)}), bf16[256,4096]{1,0:T(8,128)(2,1)}) %all-gather.10.cloned.1.call-update) | async-done | bytes 2097168 | tf_op jit(solution)/shard_map/all_gather | solution.py:131
  204.4 392.7 %all-gather.12.cloned.1.call-done = bf16[4096,8192]{1,0:T(8,128)(2,1)} async-done(((bf16[1024,8192]{1,0:T(8,128)(2,1)}), bf16[4096,8192]{1,0:T(8,128)(2,1)}) %all-gather.12.cloned.1.call-update) | async-done | bytes 67108880 | tf_op jit(solution)/shard_map/all_gather | solution.py:141
  597.1 30.6 %fusion.37 = (f32[256]{0:T(256)S(1)}, f32[256,8192]{1,0:T(8,128)}) fusion(bf16[256,4096]{1,0:T(8,128)(2,1)} %all-gather.10.cloned.1.call-done, bf16[4096,8192]{1,0:T(8,128)(2,1)} %all-gather.12.cloned.1.call-done), kind=kOutput, calls=%fused_computation.79 | convolution fusion | flops 17181966336 | bytes 77595648 | tf_op jit(solution)/shard_map/dot_general | solution.py:139
  627.7 21.3 %pmax.7 = f32[256]{0:T(256)S(1)} all-reduce(f32[256]{0:T(256)S(1)} %get-tuple-element.25), channel_id=1, replica_groups=mesh['dp'=8,'mp'=4] {'dp'}, use_global_device_ids=true, to_apply=%region_6.7 | all-reduce | flops 256 | bytes 2048 | tf_op jit(solution)/shard_map/pmax | solution.py:153
  649.0 5.1 exponential_reduce_fusion
  654.1 17.1 %all-reduce.6 = (f32[256]{0:T(256)S(1)}, f32[256]{0:T(256)S(1)}) all-reduce(f32[256]{0:T(256)S(1)} %get-tuple-element.4, f32[256]{0:T(256)S(1)} %exponential_multiply_fusion), channel_id=1, replica_groups=mesh['dp'=8,'mp'=4] {'dp'}, use_global_device_ids=true, to_apply=%region_10.11 | all-reduce | flops 512 | bytes 4096 | tf_op jit(solution)/shard_map/psum | solution.py:154
  672.0 6.0 all-reduce.7
  679.9 1.8 multiply_add_fusion
  (79 shorter events, 15.5 us)
Async XLA Ops:
  7.2 113.6 %copy-start = (bf16[4096,256]{1,0:T(8,128)(2,1)S(1)}, bf16[4096,256]{1,0:T(8,128)(2,1)}, u32[]{:S(2)}) copy-start(bf16[4096,256]{1,0:T(8,128)(2,1)} %param.22) | copy-start | bytes 6291460
  7.2 78.5 %all-gather.6.cloned.1.call-start = ((), (), s32[]{:S(2)}) async-start(), calls=%async_computation.1 | async-start | bytes 4718592 | tf_op jit(solution)/shard_map/all_gather | solution.py:62
  7.9 100.7 %all-gather.8.cloned.1.call-start = ((), (), s32[]{:S(2)}) async-start(), calls=%async_computation.2 | async-start | bytes 1310720 | tf_op jit(solution)/shard_map/all_gather | solution.py:81
  93.3 58.5 %reduce-scatter.2.cloned.1.call-start = ((), (), s32[]{:S(2)}) async-start(), calls=%async_computation.3 | async-start | bytes 1310720 | tf_op jit(solution)/shard_map/reduce_scatter | solution.py:114
  97.5 12.8 %copy-start.3 = (f32[4096]{0:T(1024)S(1)}, f32[4096]{0:T(1024)}, u32[]{:S(2)}) copy-start(f32[4096]{0:T(1024)} %param.19) | copy-start | bytes 49156
  110.2 3.0 copy-start.2
  118.2 2.6 copy-start.4
  119.5 1.4 copy-start.1
  120.8 0.7 copy-start.11
  122.9 30.2 %copy-start.5 = (f32[4096]{0:T(1024)S(1)}, f32[4096]{0:T(1024)}, u32[]{:S(2)}) copy-start(f32[4096]{0:T(1024)} %param.24) | copy-start | bytes 49156
  126.8 77.6 %all-gather.10.cloned.1.call-start = ((), (), s32[]{:S(2)}) async-start(), calls=%async_computation.4 | async-start | bytes 2359296 | tf_op jit(solution)/shard_map/all_gather | solution.py:131
  155.1 1.3 copy-start.10
  155.1 1.4 copy-start.6
  155.1 442.0 %all-gather.12.cloned.1.call-start = ((), (), s32[]{:S(2)}) async-start(), calls=%async_computation.5 | async-start | bytes 83886080 | tf_op jit(solution)/shard_map/all_gather | solution.py:141
  649.0 28.9 %copy-start.8 = (f32[22]{0:T(128)S(1)}, f32[22]{0:T(128)}, u32[]{:S(2)}) copy-start(f32[22]{0:T(128)} %param.26) | copy-start | bytes 268
  649.0 28.9 %copy-start.9 = (f32[22]{0:T(128)S(1)}, f32[22]{0:T(128)}, u32[]{:S(2)}) copy-start(f32[22]{0:T(128)} %param.27) | copy-start | bytes 268
  678.6 3.1 copy-start.7
Sparse Core Ops, SparseCore 0:
  10.1 75.5 all-gather.5
  93.4 15.2 all-gather.7
  127.0 24.7 reduce-scatter.1
  155.2 49.1 all-gather.9
  205.8 391.2 all-gather.11
where the time goes:
time: 689 us; the launch traced here: 688 us
  waiting for transfers between devices  493 us (72%)
  blocking collectives  94.2 us (14%)
  matrix products  51.6 us (7%)
  local copies, waits for them, and re-layouts  18.6 us (3%)
  between operations  15.3 us (2%)
  other arithmetic  15.2 us (2%)
    all_gather x1, waiting for transfers between devices, local(): lax.all_gather(w_vocab, 'mp', axis=0, tiled=True)  393 us
    all_gather x1, waiting for transfers between devices, local(): lax.all_gather(embedded, 'dp', axis=0, tiled=True)  58.5 us
    dot_general x1, matrix products, local(): jnp.dot(all_rows, lax.all_gather(w_vocab, 'mp', axis=0, tiled=True), pref...  30.6 us
    all_gather x1, blocking collectives, local(): lax.all_gather(targets, 'dp', axis=0, tiled=True)  26.2 us
    reduce_scatter x1, waiting for transfers between devices, local(): lax.psum_scatter(jnp.dot(mixed_heads, w_out, preferred_element_type=jnp.f...  24.9 us
    unnamed x2, blocking collectives  23.6 us
    pmax x1, blocking collectives, local(): top_all = lax.pmax(row_top, 'dp')  21.3 us
    psum x1, blocking collectives, local(): summed = lax.psum((spread * jnp.exp(row_top - top_all), picked), 'dp')  17.1 us
  transfers between devices with their start and end apart: 5, of which 5 were waited for; matrix products, arithmetic and copies ran while one was open for 2% of the time, Pallas kernels for 0%

commit v1 on v0

--- a/solution.py
+++ b/solution.py
@@ -136,11 +136,19 @@
     all_goals = everyone[1]
     all_kinds = everyone[2]
     vocab_local = w_vocab.shape[1]
-    logits = jnp.dot(
-        all_rows,
-        lax.all_gather(w_vocab, "mp", axis=0, tiled=True),
-        preferred_element_type=jnp.float32,
-    )
+
+    def try_all_map_here(shard_in, group_axis):
+        return jnp.concatenate(
+            jax.lax.all_to_all(
+                jnp.stack([shard_in for _ in range(jax.lax.axis_size(group_axis))]),
+                concat_axis=0,
+                axis_name=group_axis,
+                split_axis=0,
+            ),
+            axis=0,
+        )
+
+    logits = jnp.dot(all_rows, try_all_map_here(w_vocab, "mp"), preferred_element_type=jnp.float32)
     row_top = jnp.max(logits, axis=1)
     spread = jnp.sum(jnp.exp(logits - row_top[:, None]), axis=1)
     column_ids = all_goals - data_index * vocab_local

time: 689 us -> 874 us (1.27)
  waiting for transfers between devices: 493 us -> 644 us
  local copies, waits for them, and re-layouts: 18.6 us -> 43.5 us
  starting transfers between devices: 0.2 us -> 13.5 us
    all_to_all x0 -> x1, waiting for transfers between devices: none -> 528 us  [try_all_map_here(): jax.lax.all_to_all(jnp.stack([shard_in for _ in range(jax.lax.axis_size(g...]
    all_gather x1 -> x0, waiting for transfers between devices: 393 us -> none  [local(): lax.all_gather(w_vocab, 'mp', axis=0, tiled=True)]
    another operation x0 -> x1, local copies, waits for them, and re-layouts: none -> 26.9 us  [try_all_map_here(): jnp.stack([shard_in for _ in range(jax.lax.axis_size(group_axis))])]
    all_to_all x0 -> x1, starting transfers between devices: none -> 13.1 us  [try_all_map_here(): jax.lax.all_to_all(jnp.stack([shard_in for _ in range(jax.lax.axis_size(g...]
  transfers between devices with their start and end apart: 5 -> 5, of which waited for: 5 -> 5; matrix products, arithmetic and copies ran while one was open for 2% -> 4% of each run, Pallas kernels for 0% -> 0%
where the time goes in v1:
time: 874 us
  waiting for transfers between devices  644 us (74%)
  blocking collectives  94.8 us (11%)
  matrix products  46.9 us (5%)
  local copies, waits for them, and re-layouts  43.5 us (5%)
  other arithmetic  15.9 us (2%)
  between operations  15.3 us (2%)
  starting transfers between devices  13.5 us (2%)
    all_to_all x1, waiting for transfers between devices, try_all_map_here(): jax.lax.all_to_all(jnp.stack([shard_in for _ in range(jax.lax.axis_size(g...  528 us
    all_gather x1, waiting for transfers between devices, local(): lax.all_gather(embedded, 'dp', axis=0, tiled=True)  62.4 us
    reduce_scatter x1, waiting for transfers between devices, local(): lax.psum_scatter(jnp.dot(mixed_heads, w_out, preferred_element_type=jnp.f...  30.6 us
    dot_general x1, matrix products, local(): jnp.dot(all_rows, try_all_map_here(w_vocab, 'mp'), preferred_element_type...  30.6 us
    another operation x1, local copies, waits for them, and re-layouts, try_all_map_here(): jnp.stack([shard_in for _ in range(jax.lax.axis_size(group_axis))])  26.9 us
    all_gather x1, blocking collectives, local(): lax.all_gather(targets, 'dp', axis=0, tiled=True)  26.2 us
    unnamed x2, blocking collectives  23.3 us
    pmax x1, blocking collectives, local(): top_all = lax.pmax(row_top, 'dp')  22.5 us
  transfers between devices with their start and end apart: 5, of which 5 were waited for; matrix products, arithmetic and copies ran while one was open for 4% of the time, Pallas kernels for 0%

profile of v1, /device:TPU:0, one launch (start us, length us, event | category | flops | bytes accessed | tf_op | source)
XLA Modules:
  0.0 873.5 jit_solution(14914921144197956774)
XLA Ops:
  7.2 26.9 %stack.2 = bf16[4,1024,8192]{2,1,0:T(8,128)(2,1)} broadcast(bf16[1024,8192]{1,0:T(8,128)(2,1)} %param.25), dimensions={1,2} | broadcast | bytes 83886080 | tf_op jit(solution)/shard_map/stack | solution.py:143
  34.1 13.1 %all-to-all-start = ((bf16[4,1024,8192]{2,1,0:T(8,128)(2,1)}), bf16[4,1024,8192]{2,1,0:T(8,128)(2,1)}, u32[]{:S(2)}, u32[]{:S(2)}) async-start(bf16[4,1024,8192]{2,1,0:T(8,128)(2,1)} %stack.2), calls=%async_computation.1 | async-start | bytes 134217728 | tf_op jit(solution)/shard_map/all_to_all | solution.py:142
  50.5 13.1 %all-reduce.5 = (s32[32]{0:T(128)S(1)}, s32[32]{0:T(128)S(1)}) all-reduce(s32[32]{0:T(128)S(1)} %dynamic-update-slice, s32[32]{0:T(128)S(1)} %dynamic-update-slice.2), channel_id=1, replica_groups=mesh['dp'=8,'mp'=4] {'dp'}, use_global_device_ids=true, to_apply=%add | all-reduce | flops 64 | bytes 512
  63.8 62.4 %all-gather.5.cloned.1.call-done = bf16[32,64,1024]{2,1,0:T(8,128)(2,1)} async-done(((bf16[4,64,1024]{2,1,0:T(8,128)(2,1)}), bf16[32,64,1024]{2,1,0:T(8,128)(2,1)}) %all-gather.5.cloned.1.call-update) | async-done | bytes 4194320 | tf_op jit(solution)/shard_map/all_gather | solution.py:62
  126.2 6.8 fusion.1
  134.0 4.1 copy.67
  138.1 6.4 copy.66
  144.8 10.1 %all-gather.7.cloned.1.call-done = bf16[2,64,4096]{2,1,0:T(8,128)(2,1)} async-done(((bf16[2,64,1024]{2,1,0:T(8,128)(2,1)}), bf16[2,64,4096]{2,1,0:T(8,128)(2,1)}) %all-gather.7.cloned.1.call-update) | async-done | bytes 1048592 | tf_op jit(solution)/shard_map/all_gather | solution.py:81
  154.9 1.5 multiply_reduce_fusion
  160.5 2.6 fusion.10
  163.3 1.5 fusion.12
  166.1 3.9 convolution_convert_fusion
  170.0 30.6 %reduce-scatter.2.cloned.1.call-done = bf16[32,4096]{1,0:T(8,128)(2,1)} async-done(((bf16[128,4096]{1,0:T(8,128)(2,1)}), bf16[32,4096]{1,0:T(8,128)(2,1)}) %reduce-scatter.2.cloned.1.call-update) | async-done | bytes 262160 | tf_op jit(solution)/shard_map/reduce_scatter | solution.py:114
  202.0 2.0 multiply_convert_fusion.3
  204.8 26.2 %all-gather = s32[8,4,64]{2,1,0:T(4,128)S(1)} all-gather(s32[1,4,64]{2,1,0:T(4,128)S(1)} %bitcast.57), channel_id=1, replica_groups=mesh['dp'=8,'mp'=4] {'dp'}, dimensions={0}, use_global_device_ids=true | all-gather | bytes 9216 | tf_op jit(solution)/shard_map/all_gather | solution.py:63
  231.5 10.2 %all-reduce.4 = (s32[256]{0:T(256)S(1)}, s32[256]{0:T(256)S(1)}) all-reduce(s32[256]{0:T(256)S(1)} %dynamic-slice_dynamic-update-slice_fusion.1, s32[256]{0:T(256)S(1)} %dynamic-slice_dynamic-update-slice_fusion), channel_id=1, replica_groups=mesh['dp'=8,'mp'=4] {'dp'}, use_global_device_ids=true, to_apply=%add.1 | all-reduce | flops 512 | bytes 4096
  241.6 12.0 %all-gather.9.cloned.1.call-done = bf16[256,4096]{1,0:T(8,128)(2,1)} async-done(((bf16[32,4096]{1,0:T(8,128)(2,1)}), bf16[256,4096]{1,0:T(8,128)(2,1)}) %all-gather.9.cloned.1.call-update) | async-done | bytes 2097168 | tf_op jit(solution)/shard_map/all_gather | solution.py:131
  253.6 527.9 %all-to-all-done = bf16[4,1024,8192]{2,1,0:T(8,128)(2,1)} async-done(((bf16[4,1024,8192]{2,1,0:T(8,128)(2,1)}), bf16[4,1024,8192]{2,1,0:T(8,128)(2,1)}, u32[]{:S(2)}, u32[]{:S(2)}) %all-to-all-start) | async-done | bytes 67108896 | tf_op jit(solution)/shard_map/all_to_all | solution.py:142
  781.5 30.6 %fusion.37 = (f32[256]{0:T(256)S(1)}, f32[256,8192]{1,0:T(8,128)}) fusion(bf16[256,4096]{1,0:T(8,128)(2,1)} %all-gather.9.cloned.1.call-done, bf16[4096,8192]{1,0:T(8,128)(2,1)} %bitcast.16), kind=kOutput, calls=%fused_computation.79 | convolution fusion | flops 17181966336 | bytes 77595648 | tf_op jit(solution)/shard_map/dot_general | solution.py:151
  812.1 22.5 %pmax.7 = f32[256]{0:T(256)S(1)} all-reduce(f32[256]{0:T(256)S(1)} %get-tuple-element.25), channel_id=1, replica_groups=mesh['dp'=8,'mp'=4] {'dp'}, use_global_device_ids=true, to_apply=%region_6.7 | all-reduce | flops 256 | bytes 2048 | tf_op jit(solution)/shard_map/pmax | solution.py:161
  834.5 5.1 exponential_reduce_fusion
  839.6 17.1 %all-reduce.6 = (f32[256]{0:T(256)S(1)}, f32[256]{0:T(256)S(1)}) all-reduce(f32[256]{0:T(256)S(1)} %get-tuple-element.4, f32[256]{0:T(256)S(1)} %exponential_multiply_fusion), channel_id=1, replica_groups=mesh['dp'=8,'mp'=4] {'dp'}, use_global_device_ids=true, to_apply=%region_10.11 | all-reduce | flops 512 | bytes 4096 | tf_op jit(solution)/shard_map/psum | solution.py:162
  857.5 5.8 all-reduce.7
  865.2 1.8 multiply_add_fusion
  (83 shorter events, 14.1 us)
Async XLA Ops:
  7.2 152.1 %copy-start = (bf16[4096,256]{1,0:T(8,128)(2,1)S(1)}, bf16[4096,256]{1,0:T(8,128)(2,1)}, u32[]{:S(2)}) copy-start(bf16[4096,256]{1,0:T(8,128)(2,1)} %param.22) | copy-start | bytes 6291460
  34.1 14.0 %copy-start.13 = (u32[32]{0:T(128)S(1)}, u32[32]{0:T(128)}, u32[]{:S(2)}) copy-start(u32[32]{0:T(128)} %constant.94) | copy-start | bytes 388
  34.1 15.2 %copy-start.11 = (s32[4]{0:T(128)S(1)}, s32[4]{0:T(128)}, u32[]{:S(2)}) copy-start(s32[4]{0:T(128)} %param.18) | copy-start | bytes 52
  34.1 15.5 %copy-start.12 = (s32[4]{0:T(128)S(1)}, s32[4]{0:T(128)}, u32[]{:S(2)}) copy-start(s32[4]{0:T(128)} %param.16) | copy-start | bytes 52
  34.1 15.7 %copy-start.1 = (s32[8]{0:T(128)S(1)}, s32[8]{0:T(128)}, u32[]{:S(2)}) copy-start(s32[8]{0:T(128)} %param.17) | copy-start | bytes 100
  34.1 747.3 %all-to-all-start = ((bf16[4,1024,8192]{2,1,0:T(8,128)(2,1)}), bf16[4,1024,8192]{2,1,0:T(8,128)(2,1)}, u32[]{:S(2)}, u32[]{:S(2)}) async-start(bf16[4,1024,8192]{2,1,0:T(8,128)(2,1)} %stack.2), calls=%async_computation.1 | async-start | bytes 134217728 | tf_op jit(solution)/shard_map/all_to_all | solution.py:142
  47.3 79.0 %all-gather.5.cloned.1.call-start = ((), (), s32[]{:S(2)}) async-start(), calls=%async_computation.2 | async-start | bytes 4718592 | tf_op jit(solution)/shard_map/all_gather | solution.py:62
  48.0 106.9 %all-gather.7.cloned.1.call-start = ((), (), s32[]{:S(2)}) async-start(), calls=%async_computation.3 | async-start | bytes 1310720 | tf_op jit(solution)/shard_map/all_gather | solution.py:81
  133.8 66.9 %reduce-scatter.2.cloned.1.call-start = ((), (), s32[]{:S(2)}) async-start(), calls=%async_computation.4 | async-start | bytes 1310720 | tf_op jit(solution)/shard_map/reduce_scatter | solution.py:114
  144.8 14.5 %copy-start.5 = (f32[4096]{0:T(1024)S(1)}, f32[4096]{0:T(1024)}, u32[]{:S(2)}) copy-start(f32[4096]{0:T(1024)} %param.19) | copy-start | bytes 49156
  157.9 1.3 copy-start.2
  159.2 1.2 copy-start.3
  160.5 2.8 copy-start.4
  166.0 35.9 %copy-start.6 = (f32[4096]{0:T(1024)S(1)}, f32[4096]{0:T(1024)}, u32[]{:S(2)}) copy-start(f32[4096]{0:T(1024)} %param.24) | copy-start | bytes 49156
  170.0 34.8 %copy-start.7 = (s32[4,64]{1,0:T(4,128)S(1)}, s32[4,64]{1,0:T(4,128)}, u32[]{:S(2)}) copy-start(s32[4,64]{1,0:T(4,128)} %param.15) | copy-start | bytes 3076
  170.0 83.6 %all-gather.9.cloned.1.call-start = ((), (), s32[]{:S(2)}) async-start(), calls=%async_computation.5 | async-start | bytes 2359296 | tf_op jit(solution)/shard_map/all_gather | solution.py:131
  834.5 28.7 %copy-start.9 = (f32[22]{0:T(128)S(1)}, f32[22]{0:T(128)}, u32[]{:S(2)}) copy-start(f32[22]{0:T(128)} %param.26) | copy-start | bytes 268
  834.5 28.7 %copy-start.10 = (f32[22]{0:T(128)S(1)}, f32[22]{0:T(128)}, u32[]{:S(2)}) copy-start(f32[22]{0:T(128)} %param.27) | copy-start | bytes 268
  863.9 3.1 copy-start.8
Sparse Core Ops, SparseCore 0:
  50.2 75.9 all-gather.4
  133.9 20.9 all-gather.6
  170.1 30.4 reduce-scatter.1
  204.1 49.4 all-gather.8
